TPU v7x, 512 devices: a whole 4x8x8 slice. The times are simulated.
512 devices in a mesh: gx: 32 (over y_hi, z, core), yz: 16 (over x, y_lo).
Axes of the slice: x: 4, y: 8 (y_hi: 2, y_lo: 4; y = y_hi * 4 + y_lo), z: 8, core: 2. Of those that a mesh axis runs over, the one named last changes fastest.
Arguments:
- gauge_links: float32 [64, 2, 3, 3, 2048], P('gx', None, None, None, 'yz'), may hold values from -1 to 1, as said below
- in_field: float32 [8, 64, 2, 3, 3, 2048], P(None, 'gx', None, None, None, 'yz'), may hold values from -6 to 6
- cotangent: float32 [8, 64, 2, 3, 3, 2048], P(None, 'gx', None, None, None, 'yz'), may hold values from -6 to 6
- bilinear_weights: float32 [8, 8, 24, 8], replicated, may hold values from -0.15625 to 0.15625
Outputs:
- grad_field: float32 [8, 64, 2, 3, 3, 2048], P(None, 'gx', None, None, None, 'yz')
- grad_weights: float32 [8, 8, 24, 8], replicated
Inputs may be any that keep to these rules, and one draw needn't show every extreme that they name: `gauge_links`: every site's link is a special unitary 3 x 3 matrix (unitary with determinant 1), stored as real and imaginary parts.
All inputs are finite; a program needn't handle non-finite values.
Results may differ from a plain program's by a relative error of at most 0.0003.
Values sent between devices are 32-bit elements; how exact they have to be, the bound alone decides.
No kernel may reach another device: no remote copies, remote signals or barrier semaphores. Data moves between devices by JAX's collectives and lax.ppermute only.
A program may use at most 64 MiB of HBM per device.

v0:
```python
import math
import jax
import jax.numpy as jnp
from jax import lax
from jax.sharding import PartitionSpec as P


def from_behind(block, axis, distance):
    devices = range(lax.axis_size(axis))
    route = [((i - distance) % len(devices), i) for i in devices]
    return lax.ppermute(block, axis, route)


def matmul_three(left, right):
    return jnp.sum(left[..., :, :, None, :] * right[..., None, :, :, :], axis=-3)


def complex_mul(left, right):
    left_re = left[..., 0, :, :, :]
    left_im = left[..., 1, :, :, :]
    right_re = right[..., 0, :, :, :]
    right_im = right[..., 1, :, :, :]
    real_part = matmul_three(left_re, right_re) - matmul_three(left_im, right_im)
    imag_part = matmul_three(left_re, right_im) + matmul_three(left_im, right_re)
    return jnp.stack([real_part, imag_part], axis=-4)


def dagger(matrix):
    swapped = jnp.swapaxes(matrix, -3, -2)
    return jnp.stack([swapped[..., 0, :, :, :], -swapped[..., 1, :, :, :]], axis=-4)


def per_device(gauge_links, in_field, cotangent, bilinear_weights):
    part_x = gauge_links.shape[0]
    channels = in_field.shape[0]
    line_count = bilinear_weights.shape[2]
    site_count = gauge_links.shape[-1]
    reach_devs = (part_x - 1 + line_count) // part_x
    highest = lax.Precision.HIGHEST
    weight_rows = bilinear_weights.reshape(channels * channels, line_count * channels)

    def advance(carry, unused):
        arrived = from_behind(carry, "gx", -1)
        return (arrived, arrived)

    unused_last, stacked = lax.scan(advance, (gauge_links, in_field), None, length=reach_devs)
    window_links = jnp.concatenate(
        [gauge_links, stacked[0].reshape((-1, 2, 3, 3, site_count))], axis=0
    )
    later_field = jnp.moveaxis(stacked[1], 0, 1).reshape((channels, -1, 2, 3, 3, site_count))
    window_field = jnp.concatenate([in_field, later_field], axis=1)
    pair_grad = complex_mul(dagger(in_field)[None], cotangent[:, None]).reshape(
        channels * channels, -1
    )

    def forward_step(line, offset):
        shifted = lax.dynamic_slice_in_dim(window_field, offset, part_x, axis=1)
        transported = complex_mul(complex_mul(line[None], shifted), dagger(line)[None])
        next_links = lax.dynamic_slice_in_dim(window_links, offset, part_x, axis=0)
        return (complex_mul(line, next_links), (transported, line))

    offsets = jnp.arange(1, line_count + 1, dtype=jnp.int32)
    unused_line, (all_transported, all_lines) = lax.scan(forward_step, gauge_links, offsets)
    transported_flat = all_transported.reshape(line_count * channels, -1)
    partial_grad = lax.dot_general(
        pair_grad, transported_flat, (((1,), (1,)), ((), ())), precision=highest
    )
    mixed = jnp.dot(weight_rows, transported_flat, precision=highest)
    mixed_matrix = mixed.reshape((channels, channels) + in_field.shape[1:])
    direct = jnp.sum(complex_mul(cotangent[:, None], dagger(mixed_matrix)), axis=0)
    line_grad = jnp.dot(weight_rows.T, pair_grad, precision=highest)
    line_grad = line_grad.reshape((line_count,) + in_field.shape)
    accumulator = jnp.zeros((channels, (reach_devs + 1) * part_x, 2, 3, 3, site_count), jnp.float32)

    def backward_step(carry, inputs):
        offset, grad_piece, line = inputs
        contribution = complex_mul(complex_mul(dagger(line)[None], grad_piece), line[None])
        current = lax.dynamic_slice_in_dim(carry, offset, part_x, axis=1)
        return (
            lax.dynamic_update_slice_in_dim(carry, current + contribution, offset, axis=1),
            None,
        )

    accumulator, unused_out = lax.scan(backward_step, accumulator, (offsets, line_grad, all_lines))
    blocks = jnp.moveaxis(
        accumulator.reshape((channels, reach_devs + 1, part_x, 2, 3, 3, site_count)), 1, 0
    )

    def return_step(carry, block):
        arrived = from_behind(carry, "gx", 1)
        return (arrived + block, None)

    far_terms, unused_tail = lax.scan(return_step, blocks[reach_devs], blocks[:reach_devs][::-1])
    grad_field = direct + far_terms
    total_x = part_x * lax.axis_size("gx")
    total_sites = site_count * lax.axis_size("yz")
    summed = lax.psum(partial_grad, ("gx", "yz"))
    grad_weights = summed.reshape(channels, channels, line_count, channels) / math.sqrt(
        100.0 * total_x * total_sites
    )
    return (grad_field, grad_weights)


def solution(mesh):
    placed = (
        P("gx", None, None, None, "yz"),
        P(None, "gx", None, None, None, "yz"),
        P(None, "gx", None, None, None, "yz"),
        P(),
    )
    return jax.shard_map(
        per_device,
        mesh=mesh,
        in_specs=placed,
        out_specs=(P(None, "gx", None, None, None, "yz"), P()),
        check_vma=False,
    )
```

profile of v0, /device:TPU:2, one launch (start us, length us, event | category | flops | bytes accessed | tf_op | source)
XLA Modules:
  0.0 771.0 jit_solution(7964423564091880756)
XLA Ops:
  2.4 183.7 %while.50 = (s32[]{:T(128)}, f32[2,2,3,3,128]{4,1,3,2,0:T(2,128)S(1)}, f32[8,2,2,3,3,128]{5,2,4,3,1,0:T(2,128)S(1)}, f32[12,2,2,3,3,128]{5,1,0,4,3,2:T(2,128)S(1...) while((s32[]{:T(128)}, f32[2,2,3,3,128]{4,1,3,2,0:T(2,128)S(1)}, ...), condition=%wide.region_1.2_spmd, body=%wide.region_0.1_spmd.sunk | while | flops 2 | bytes 1327269 | solution.py:46
  2.4 15.6 %collective-permute-start = (f32[2,2,3,3,128]{4,1,3,2,0:T(2,128)S(1)}, f32[2,2,3,3,128]{4,1,3,2,0:T(2,128)S(1)}, u32[]{:S(2)}, u32[]{:S(2)}) collective-permute-start(f32[2,2,3,3,128]{4,1,3,2,0:T(2,128)S(1)} %get-tuple-element.507), channel_id=1, source_target_pairs={{16,0},{32,16},{48,32},{64,48},{80,64},{96,80},{112,96},{128,112},... | collective-permute-start | bytes 55304 | tf_op jit(solution)/shard_map/while/body/eval_jaxpr/ppermute | solution.py:11
  20.6 4.2 collective-permute-done.1
  24.9 9.8 %collective-permute-start = (f32[2,2,3,3,128]{4,1,3,2,0:T(2,128)S(1)}, f32[2,2,3,3,128]{4,1,3,2,0:T(2,128)S(1)}, u32[]{:S(2)}, u32[]{:S(2)}) collective-permute-start(f32[2,2,3,3,128]{4,1,3,2,0:T(2,128)S(1)} %get-tuple-element.507), channel_id=1, source_target_pairs={{16,0},{32,16},{48,32},{64,48},{80,64},{96,80},{112,96},{128,112},... | collective-permute-start | bytes 55304 | tf_op jit(solution)/shard_map/while/body/eval_jaxpr/ppermute | solution.py:11
  40.8 9.8 %collective-permute-start = (f32[2,2,3,3,128]{4,1,3,2,0:T(2,128)S(1)}, f32[2,2,3,3,128]{4,1,3,2,0:T(2,128)S(1)}, u32[]{:S(2)}, u32[]{:S(2)}) collective-permute-start(f32[2,2,3,3,128]{4,1,3,2,0:T(2,128)S(1)} %get-tuple-element.507), channel_id=1, source_target_pairs={{16,0},{32,16},{48,32},{64,48},{80,64},{96,80},{112,96},{128,112},... | collective-permute-start | bytes 55304 | tf_op jit(solution)/shard_map/while/body/eval_jaxpr/ppermute | solution.py:11
  55.4 9.8 %collective-permute-start = (f32[2,2,3,3,128]{4,1,3,2,0:T(2,128)S(1)}, f32[2,2,3,3,128]{4,1,3,2,0:T(2,128)S(1)}, u32[]{:S(2)}, u32[]{:S(2)}) collective-permute-start(f32[2,2,3,3,128]{4,1,3,2,0:T(2,128)S(1)} %get-tuple-element.507), channel_id=1, source_target_pairs={{16,0},{32,16},{48,32},{64,48},{80,64},{96,80},{112,96},{128,112},... | collective-permute-start | bytes 55304 | tf_op jit(solution)/shard_map/while/body/eval_jaxpr/ppermute | solution.py:11
  69.9 9.8 %collective-permute-start = (f32[2,2,3,3,128]{4,1,3,2,0:T(2,128)S(1)}, f32[2,2,3,3,128]{4,1,3,2,0:T(2,128)S(1)}, u32[]{:S(2)}, u32[]{:S(2)}) collective-permute-start(f32[2,2,3,3,128]{4,1,3,2,0:T(2,128)S(1)} %get-tuple-element.507), channel_id=1, source_target_pairs={{16,0},{32,16},{48,32},{64,48},{80,64},{96,80},{112,96},{128,112},... | collective-permute-start | bytes 55304 | tf_op jit(solution)/shard_map/while/body/eval_jaxpr/ppermute | solution.py:11
  84.4 9.8 %collective-permute-start = (f32[2,2,3,3,128]{4,1,3,2,0:T(2,128)S(1)}, f32[2,2,3,3,128]{4,1,3,2,0:T(2,128)S(1)}, u32[]{:S(2)}, u32[]{:S(2)}) collective-permute-start(f32[2,2,3,3,128]{4,1,3,2,0:T(2,128)S(1)} %get-tuple-element.507), channel_id=1, source_target_pairs={{16,0},{32,16},{48,32},{64,48},{80,64},{96,80},{112,96},{128,112},... | collective-permute-start | bytes 55304 | tf_op jit(solution)/shard_map/while/body/eval_jaxpr/ppermute | solution.py:11
  99.0 9.8 %collective-permute-start = (f32[2,2,3,3,128]{4,1,3,2,0:T(2,128)S(1)}, f32[2,2,3,3,128]{4,1,3,2,0:T(2,128)S(1)}, u32[]{:S(2)}, u32[]{:S(2)}) collective-permute-start(f32[2,2,3,3,128]{4,1,3,2,0:T(2,128)S(1)} %get-tuple-element.507), channel_id=1, source_target_pairs={{16,0},{32,16},{48,32},{64,48},{80,64},{96,80},{112,96},{128,112},... | collective-permute-start | bytes 55304 | tf_op jit(solution)/shard_map/while/body/eval_jaxpr/ppermute | solution.py:11
  113.5 9.8 %collective-permute-start = (f32[2,2,3,3,128]{4,1,3,2,0:T(2,128)S(1)}, f32[2,2,3,3,128]{4,1,3,2,0:T(2,128)S(1)}, u32[]{:S(2)}, u32[]{:S(2)}) collective-permute-start(f32[2,2,3,3,128]{4,1,3,2,0:T(2,128)S(1)} %get-tuple-element.507), channel_id=1, source_target_pairs={{16,0},{32,16},{48,32},{64,48},{80,64},{96,80},{112,96},{128,112},... | collective-permute-start | bytes 55304 | tf_op jit(solution)/shard_map/while/body/eval_jaxpr/ppermute | solution.py:11
  128.0 9.8 %collective-permute-start = (f32[2,2,3,3,128]{4,1,3,2,0:T(2,128)S(1)}, f32[2,2,3,3,128]{4,1,3,2,0:T(2,128)S(1)}, u32[]{:S(2)}, u32[]{:S(2)}) collective-permute-start(f32[2,2,3,3,128]{4,1,3,2,0:T(2,128)S(1)} %get-tuple-element.507), channel_id=1, source_target_pairs={{16,0},{32,16},{48,32},{64,48},{80,64},{96,80},{112,96},{128,112},... | collective-permute-start | bytes 55304 | tf_op jit(solution)/shard_map/while/body/eval_jaxpr/ppermute | solution.py:11
  142.5 9.8 %collective-permute-start = (f32[2,2,3,3,128]{4,1,3,2,0:T(2,128)S(1)}, f32[2,2,3,3,128]{4,1,3,2,0:T(2,128)S(1)}, u32[]{:S(2)}, u32[]{:S(2)}) collective-permute-start(f32[2,2,3,3,128]{4,1,3,2,0:T(2,128)S(1)} %get-tuple-element.507), channel_id=1, source_target_pairs={{16,0},{32,16},{48,32},{64,48},{80,64},{96,80},{112,96},{128,112},... | collective-permute-start | bytes 55304 | tf_op jit(solution)/shard_map/while/body/eval_jaxpr/ppermute | solution.py:11
  157.0 9.8 %collective-permute-start = (f32[2,2,3,3,128]{4,1,3,2,0:T(2,128)S(1)}, f32[2,2,3,3,128]{4,1,3,2,0:T(2,128)S(1)}, u32[]{:S(2)}, u32[]{:S(2)}) collective-permute-start(f32[2,2,3,3,128]{4,1,3,2,0:T(2,128)S(1)} %get-tuple-element.507), channel_id=1, source_target_pairs={{16,0},{32,16},{48,32},{64,48},{80,64},{96,80},{112,96},{128,112},... | collective-permute-start | bytes 55304 | tf_op jit(solution)/shard_map/while/body/eval_jaxpr/ppermute | solution.py:11
  171.6 9.8 %collective-permute-start = (f32[2,2,3,3,128]{4,1,3,2,0:T(2,128)S(1)}, f32[2,2,3,3,128]{4,1,3,2,0:T(2,128)S(1)}, u32[]{:S(2)}, u32[]{:S(2)}) collective-permute-start(f32[2,2,3,3,128]{4,1,3,2,0:T(2,128)S(1)} %get-tuple-element.507), channel_id=1, source_target_pairs={{16,0},{32,16},{48,32},{64,48},{80,64},{96,80},{112,96},{128,112},... | collective-permute-start | bytes 55304 | tf_op jit(solution)/shard_map/while/body/eval_jaxpr/ppermute | solution.py:11
  189.8 184.4 %while.51 = (s32[]{:T(128)}, f32[2,2,3,3,128]{4,0,3,2,1:T(2,128)}, f32[24,8,2,2,3,3,128]{6,1,5,4,3,2,0:T(8,128)S(1)}, f32[24,2,2,3,3,128]{5,1,4,3,2,0:T(2,128)},...) while((s32[]{:T(128)}, f32[2,2,3,3,128]{4,0,3,2,1:T(2,128)}, ...), condition=%wide.region_15.16_spmd, body=%wide.region_2.15_spmd.sunk | while | flops 910086 | bytes 2968279 | solution.py:63
  387.9 4.2 fusion.7
  392.1 100.0 %psum.7 = f32[64,192]{1,0:T(8,128)S(1)} all-reduce(f32[64,192]{1,0:T(8,128)} %fusion.7), channel_id=1, replica_groups=mesh['gx'=32,'yz'=16] {'gx','yz'}, use_global_device_ids=true, to_apply=%region_37.38 | all-reduce | flops 12288 | bytes 98304 | tf_op jit(solution)/shard_map/psum | solution.py:97
  493.3 4.7 fusion.6
  498.1 104.9 %while.52 = (s32[]{:T(128)}, f32[8,26,2,3,3,128]{5,0,4,3,2,1:T(8,128)S(1)}, s32[24]{0:T(128)S(1)}, f32[24,2,2,3,3,128]{5,1,4,3,2,0:T(2,128)}, f32[24,8,2,2,3,3,1...) while((s32[]{:T(128)}, f32[8,26,2,3,3,128]{5,0,4,3,2,1:T(8,128)S(1)}, s32[24]{0:T(128)S(1)}, ...), condition=%wide.region_34.35_spmd, body=%wide.region_25.34_spmd.sunk | while | flops 891653 | bytes 3411083 | solution.py:84
  607.3 161.5 %while.53 = (s32[]{:T(128)}, f32[8,2,2,3,3,128]{5,4,3,2,1,0:T(4,128)S(1)}, f32[12,8,2,2,3,3,128]{6,1,5,4,3,2,0:T(8,128)}, s32[]{:T(128)}) while((s32[]{:T(128)}, f32[8,2,2,3,3,128]{5,4,3,2,1,0:T(4,128)S(1)}, f32[12,8,2,2,3,3,128]{6,1,5,4,3,2,0:T(8,128)}, s32[]{:T(128)}) %tuple.163), condition=%wide.region_36.37_spmd, body=%wide.region_35.36_spmd.sunk | while | flops 36866 | bytes 1327209 | solution.py:93
  610.3 12.3 %collective-permute-done.2 = f32[8,2,2,3,3,128]{5,4,3,2,1,0:T(4,128)S(1)} collective-permute-done((f32[8,2,2,3,3,128]{5,4,3,2,1,0:T(4,128)S(1)}, f32[8,2,2,3,3,128]{5,4,3,2,1,0:T(4,128)S(1)}, u32[]{:S(2)}, u32[]{:S(2)}) %collective-permute-start.2) | collective-permute-done | bytes 147488 | tf_op jit(solution)/shard_map/while/body/eval_jaxpr/ppermute | solution.py:11
  625.5 12.2 %collective-permute-done.2 = f32[8,2,2,3,3,128]{5,4,3,2,1,0:T(4,128)S(1)} collective-permute-done((f32[8,2,2,3,3,128]{5,4,3,2,1,0:T(4,128)S(1)}, f32[8,2,2,3,3,128]{5,4,3,2,1,0:T(4,128)S(1)}, u32[]{:S(2)}, u32[]{:S(2)}) %collective-permute-start.2) | collective-permute-done | bytes 147488 | tf_op jit(solution)/shard_map/while/body/eval_jaxpr/ppermute | solution.py:11
  640.7 10.2 %collective-permute-done.2 = f32[8,2,2,3,3,128]{5,4,3,2,1,0:T(4,128)S(1)} collective-permute-done((f32[8,2,2,3,3,128]{5,4,3,2,1,0:T(4,128)S(1)}, f32[8,2,2,3,3,128]{5,4,3,2,1,0:T(4,128)S(1)}, u32[]{:S(2)}, u32[]{:S(2)}) %collective-permute-start.2) | collective-permute-done | bytes 147488 | tf_op jit(solution)/shard_map/while/body/eval_jaxpr/ppermute | solution.py:11
  653.9 10.2 %collective-permute-done.2 = f32[8,2,2,3,3,128]{5,4,3,2,1,0:T(4,128)S(1)} collective-permute-done((f32[8,2,2,3,3,128]{5,4,3,2,1,0:T(4,128)S(1)}, f32[8,2,2,3,3,128]{5,4,3,2,1,0:T(4,128)S(1)}, u32[]{:S(2)}, u32[]{:S(2)}) %collective-permute-start.2) | collective-permute-done | bytes 147488 | tf_op jit(solution)/shard_map/while/body/eval_jaxpr/ppermute | solution.py:11
  667.0 10.1 %collective-permute-done.2 = f32[8,2,2,3,3,128]{5,4,3,2,1,0:T(4,128)S(1)} collective-permute-done((f32[8,2,2,3,3,128]{5,4,3,2,1,0:T(4,128)S(1)}, f32[8,2,2,3,3,128]{5,4,3,2,1,0:T(4,128)S(1)}, u32[]{:S(2)}, u32[]{:S(2)}) %collective-permute-start.2) | collective-permute-done | bytes 147488 | tf_op jit(solution)/shard_map/while/body/eval_jaxpr/ppermute | solution.py:11
  680.1 10.1 %collective-permute-done.2 = f32[8,2,2,3,3,128]{5,4,3,2,1,0:T(4,128)S(1)} collective-permute-done((f32[8,2,2,3,3,128]{5,4,3,2,1,0:T(4,128)S(1)}, f32[8,2,2,3,3,128]{5,4,3,2,1,0:T(4,128)S(1)}, u32[]{:S(2)}, u32[]{:S(2)}) %collective-permute-start.2) | collective-permute-done | bytes 147488 | tf_op jit(solution)/shard_map/while/body/eval_jaxpr/ppermute | solution.py:11
  693.2 10.1 %collective-permute-done.2 = f32[8,2,2,3,3,128]{5,4,3,2,1,0:T(4,128)S(1)} collective-permute-done((f32[8,2,2,3,3,128]{5,4,3,2,1,0:T(4,128)S(1)}, f32[8,2,2,3,3,128]{5,4,3,2,1,0:T(4,128)S(1)}, u32[]{:S(2)}, u32[]{:S(2)}) %collective-permute-start.2) | collective-permute-done | bytes 147488 | tf_op jit(solution)/shard_map/while/body/eval_jaxpr/ppermute | solution.py:11
  706.3 10.1 %collective-permute-done.2 = f32[8,2,2,3,3,128]{5,4,3,2,1,0:T(4,128)S(1)} collective-permute-done((f32[8,2,2,3,3,128]{5,4,3,2,1,0:T(4,128)S(1)}, f32[8,2,2,3,3,128]{5,4,3,2,1,0:T(4,128)S(1)}, u32[]{:S(2)}, u32[]{:S(2)}) %collective-permute-start.2) | collective-permute-done | bytes 147488 | tf_op jit(solution)/shard_map/while/body/eval_jaxpr/ppermute | solution.py:11
  719.4 10.1 %collective-permute-done.2 = f32[8,2,2,3,3,128]{5,4,3,2,1,0:T(4,128)S(1)} collective-permute-done((f32[8,2,2,3,3,128]{5,4,3,2,1,0:T(4,128)S(1)}, f32[8,2,2,3,3,128]{5,4,3,2,1,0:T(4,128)S(1)}, u32[]{:S(2)}, u32[]{:S(2)}) %collective-permute-start.2) | collective-permute-done | bytes 147488 | tf_op jit(solution)/shard_map/while/body/eval_jaxpr/ppermute | solution.py:11
  732.5 10.1 %collective-permute-done.2 = f32[8,2,2,3,3,128]{5,4,3,2,1,0:T(4,128)S(1)} collective-permute-done((f32[8,2,2,3,3,128]{5,4,3,2,1,0:T(4,128)S(1)}, f32[8,2,2,3,3,128]{5,4,3,2,1,0:T(4,128)S(1)}, u32[]{:S(2)}, u32[]{:S(2)}) %collective-permute-start.2) | collective-permute-done | bytes 147488 | tf_op jit(solution)/shard_map/while/body/eval_jaxpr/ppermute | solution.py:11
  745.6 10.1 %collective-permute-done.2 = f32[8,2,2,3,3,128]{5,4,3,2,1,0:T(4,128)S(1)} collective-permute-done((f32[8,2,2,3,3,128]{5,4,3,2,1,0:T(4,128)S(1)}, f32[8,2,2,3,3,128]{5,4,3,2,1,0:T(4,128)S(1)}, u32[]{:S(2)}, u32[]{:S(2)}) %collective-permute-start.2) | collective-permute-done | bytes 147488 | tf_op jit(solution)/shard_map/while/body/eval_jaxpr/ppermute | solution.py:11
  758.7 10.1 %collective-permute-done.2 = f32[8,2,2,3,3,128]{5,4,3,2,1,0:T(4,128)S(1)} collective-permute-done((f32[8,2,2,3,3,128]{5,4,3,2,1,0:T(4,128)S(1)}, f32[8,2,2,3,3,128]{5,4,3,2,1,0:T(4,128)S(1)}, u32[]{:S(2)}, u32[]{:S(2)}) %collective-permute-start.2) | collective-permute-done | bytes 147488 | tf_op jit(solution)/shard_map/while/body/eval_jaxpr/ppermute | solution.py:11
  (1213 shorter events, 310.5 us)
Async XLA Ops:
  2.4 18.2 %collective-permute-start = (f32[2,2,3,3,128]{4,1,3,2,0:T(2,128)S(1)}, f32[2,2,3,3,128]{4,1,3,2,0:T(2,128)S(1)}, u32[]{:S(2)}, u32[]{:S(2)}) collective-permute-start(f32[2,2,3,3,128]{4,1,3,2,0:T(2,128)S(1)} %get-tuple-element.507), channel_id=1, source_target_pairs={{16,0},{32,16},{48,32},{64,48},{80,64},{96,80},{112,96},{128,112},... | collective-permute-start | bytes 55304 | tf_op jit(solution)/shard_map/while/body/eval_jaxpr/ppermute | solution.py:11
  18.0 6.8 collective-permute-start.1
  24.9 11.7 %collective-permute-start = (f32[2,2,3,3,128]{4,1,3,2,0:T(2,128)S(1)}, f32[2,2,3,3,128]{4,1,3,2,0:T(2,128)S(1)}, u32[]{:S(2)}, u32[]{:S(2)}) collective-permute-start(f32[2,2,3,3,128]{4,1,3,2,0:T(2,128)S(1)} %get-tuple-element.507), channel_id=1, source_target_pairs={{16,0},{32,16},{48,32},{64,48},{80,64},{96,80},{112,96},{128,112},... | collective-permute-start | bytes 55304 | tf_op jit(solution)/shard_map/while/body/eval_jaxpr/ppermute | solution.py:11
  34.7 5.9 collective-permute-start.1
  40.8 11.8 %collective-permute-start = (f32[2,2,3,3,128]{4,1,3,2,0:T(2,128)S(1)}, f32[2,2,3,3,128]{4,1,3,2,0:T(2,128)S(1)}, u32[]{:S(2)}, u32[]{:S(2)}) collective-permute-start(f32[2,2,3,3,128]{4,1,3,2,0:T(2,128)S(1)} %get-tuple-element.507), channel_id=1, source_target_pairs={{16,0},{32,16},{48,32},{64,48},{80,64},{96,80},{112,96},{128,112},... | collective-permute-start | bytes 55304 | tf_op jit(solution)/shard_map/while/body/eval_jaxpr/ppermute | solution.py:11
  50.6 4.7 collective-permute-start.1
  55.4 11.8 %collective-permute-start = (f32[2,2,3,3,128]{4,1,3,2,0:T(2,128)S(1)}, f32[2,2,3,3,128]{4,1,3,2,0:T(2,128)S(1)}, u32[]{:S(2)}, u32[]{:S(2)}) collective-permute-start(f32[2,2,3,3,128]{4,1,3,2,0:T(2,128)S(1)} %get-tuple-element.507), channel_id=1, source_target_pairs={{16,0},{32,16},{48,32},{64,48},{80,64},{96,80},{112,96},{128,112},... | collective-permute-start | bytes 55304 | tf_op jit(solution)/shard_map/while/body/eval_jaxpr/ppermute | solution.py:11
  65.2 4.6 collective-permute-start.1
  69.9 11.8 %collective-permute-start = (f32[2,2,3,3,128]{4,1,3,2,0:T(2,128)S(1)}, f32[2,2,3,3,128]{4,1,3,2,0:T(2,128)S(1)}, u32[]{:S(2)}, u32[]{:S(2)}) collective-permute-start(f32[2,2,3,3,128]{4,1,3,2,0:T(2,128)S(1)} %get-tuple-element.507), channel_id=1, source_target_pairs={{16,0},{32,16},{48,32},{64,48},{80,64},{96,80},{112,96},{128,112},... | collective-permute-start | bytes 55304 | tf_op jit(solution)/shard_map/while/body/eval_jaxpr/ppermute | solution.py:11
  79.8 4.6 collective-permute-start.1
  84.4 11.8 %collective-permute-start = (f32[2,2,3,3,128]{4,1,3,2,0:T(2,128)S(1)}, f32[2,2,3,3,128]{4,1,3,2,0:T(2,128)S(1)}, u32[]{:S(2)}, u32[]{:S(2)}) collective-permute-start(f32[2,2,3,3,128]{4,1,3,2,0:T(2,128)S(1)} %get-tuple-element.507), channel_id=1, source_target_pairs={{16,0},{32,16},{48,32},{64,48},{80,64},{96,80},{112,96},{128,112},... | collective-permute-start | bytes 55304 | tf_op jit(solution)/shard_map/while/body/eval_jaxpr/ppermute | solution.py:11
  94.3 4.6 collective-permute-start.1
  99.0 11.8 %collective-permute-start = (f32[2,2,3,3,128]{4,1,3,2,0:T(2,128)S(1)}, f32[2,2,3,3,128]{4,1,3,2,0:T(2,128)S(1)}, u32[]{:S(2)}, u32[]{:S(2)}) collective-permute-start(f32[2,2,3,3,128]{4,1,3,2,0:T(2,128)S(1)} %get-tuple-element.507), channel_id=1, source_target_pairs={{16,0},{32,16},{48,32},{64,48},{80,64},{96,80},{112,96},{128,112},... | collective-permute-start | bytes 55304 | tf_op jit(solution)/shard_map/while/body/eval_jaxpr/ppermute | solution.py:11
  108.8 4.6 collective-permute-start.1
  113.5 11.8 %collective-permute-start = (f32[2,2,3,3,128]{4,1,3,2,0:T(2,128)S(1)}, f32[2,2,3,3,128]{4,1,3,2,0:T(2,128)S(1)}, u32[]{:S(2)}, u32[]{:S(2)}) collective-permute-start(f32[2,2,3,3,128]{4,1,3,2,0:T(2,128)S(1)} %get-tuple-element.507), channel_id=1, source_target_pairs={{16,0},{32,16},{48,32},{64,48},{80,64},{96,80},{112,96},{128,112},... | collective-permute-start | bytes 55304 | tf_op jit(solution)/shard_map/while/body/eval_jaxpr/ppermute | solution.py:11
  128.0 11.8 %collective-permute-start = (f32[2,2,3,3,128]{4,1,3,2,0:T(2,128)S(1)}, f32[2,2,3,3,128]{4,1,3,2,0:T(2,128)S(1)}, u32[]{:S(2)}, u32[]{:S(2)}) collective-permute-start(f32[2,2,3,3,128]{4,1,3,2,0:T(2,128)S(1)} %get-tuple-element.507), channel_id=1, source_target_pairs={{16,0},{32,16},{48,32},{64,48},{80,64},{96,80},{112,96},{128,112},... | collective-permute-start | bytes 55304 | tf_op jit(solution)/shard_map/while/body/eval_jaxpr/ppermute | solution.py:11
  142.5 11.8 %collective-permute-start = (f32[2,2,3,3,128]{4,1,3,2,0:T(2,128)S(1)}, f32[2,2,3,3,128]{4,1,3,2,0:T(2,128)S(1)}, u32[]{:S(2)}, u32[]{:S(2)}) collective-permute-start(f32[2,2,3,3,128]{4,1,3,2,0:T(2,128)S(1)} %get-tuple-element.507), channel_id=1, source_target_pairs={{16,0},{32,16},{48,32},{64,48},{80,64},{96,80},{112,96},{128,112},... | collective-permute-start | bytes 55304 | tf_op jit(solution)/shard_map/while/body/eval_jaxpr/ppermute | solution.py:11
  152.3 4.6 collective-permute-start.1
  157.0 11.8 %collective-permute-start = (f32[2,2,3,3,128]{4,1,3,2,0:T(2,128)S(1)}, f32[2,2,3,3,128]{4,1,3,2,0:T(2,128)S(1)}, u32[]{:S(2)}, u32[]{:S(2)}) collective-permute-start(f32[2,2,3,3,128]{4,1,3,2,0:T(2,128)S(1)} %get-tuple-element.507), channel_id=1, source_target_pairs={{16,0},{32,16},{48,32},{64,48},{80,64},{96,80},{112,96},{128,112},... | collective-permute-start | bytes 55304 | tf_op jit(solution)/shard_map/while/body/eval_jaxpr/ppermute | solution.py:11
  171.6 11.8 %collective-permute-start = (f32[2,2,3,3,128]{4,1,3,2,0:T(2,128)S(1)}, f32[2,2,3,3,128]{4,1,3,2,0:T(2,128)S(1)}, u32[]{:S(2)}, u32[]{:S(2)}) collective-permute-start(f32[2,2,3,3,128]{4,1,3,2,0:T(2,128)S(1)} %get-tuple-element.507), channel_id=1, source_target_pairs={{16,0},{32,16},{48,32},{64,48},{80,64},{96,80},{112,96},{128,112},... | collective-permute-start | bytes 55304 | tf_op jit(solution)/shard_map/while/body/eval_jaxpr/ppermute | solution.py:11
  607.3 15.2 %collective-permute-start.2 = (f32[8,2,2,3,3,128]{5,4,3,2,1,0:T(4,128)S(1)}, f32[8,2,2,3,3,128]{5,4,3,2,1,0:T(4,128)S(1)}, u32[]{:S(2)}, u32[]{:S(2)}) collective-permute-start(f32[8,2,2,3,3,128]{5,4,3,2,1,0:T(4,128)S(1)} %get-tuple-element.580), channel_id=1, source_target_pairs={{496,0},{0,16},{16,32},{32,48},{48,64},{64,80},{80,96},{96,112},{1... | collective-permute-start | bytes 442376 | tf_op jit(solution)/shard_map/while/body/eval_jaxpr/ppermute | solution.py:11
  622.7 15.1 %collective-permute-start.2 = (f32[8,2,2,3,3,128]{5,4,3,2,1,0:T(4,128)S(1)}, f32[8,2,2,3,3,128]{5,4,3,2,1,0:T(4,128)S(1)}, u32[]{:S(2)}, u32[]{:S(2)}) collective-permute-start(f32[8,2,2,3,3,128]{5,4,3,2,1,0:T(4,128)S(1)} %get-tuple-element.580), channel_id=1, source_target_pairs={{496,0},{0,16},{16,32},{32,48},{48,64},{64,80},{80,96},{96,112},{1... | collective-permute-start | bytes 442376 | tf_op jit(solution)/shard_map/while/body/eval_jaxpr/ppermute | solution.py:11
  637.9 13.1 %collective-permute-start.2 = (f32[8,2,2,3,3,128]{5,4,3,2,1,0:T(4,128)S(1)}, f32[8,2,2,3,3,128]{5,4,3,2,1,0:T(4,128)S(1)}, u32[]{:S(2)}, u32[]{:S(2)}) collective-permute-start(f32[8,2,2,3,3,128]{5,4,3,2,1,0:T(4,128)S(1)} %get-tuple-element.580), channel_id=1, source_target_pairs={{496,0},{0,16},{16,32},{32,48},{48,64},{64,80},{80,96},{96,112},{1... | collective-permute-start | bytes 442376 | tf_op jit(solution)/shard_map/while/body/eval_jaxpr/ppermute | solution.py:11
  651.1 13.0 %collective-permute-start.2 = (f32[8,2,2,3,3,128]{5,4,3,2,1,0:T(4,128)S(1)}, f32[8,2,2,3,3,128]{5,4,3,2,1,0:T(4,128)S(1)}, u32[]{:S(2)}, u32[]{:S(2)}) collective-permute-start(f32[8,2,2,3,3,128]{5,4,3,2,1,0:T(4,128)S(1)} %get-tuple-element.580), channel_id=1, source_target_pairs={{496,0},{0,16},{16,32},{32,48},{48,64},{64,80},{80,96},{96,112},{1... | collective-permute-start | bytes 442376 | tf_op jit(solution)/shard_map/while/body/eval_jaxpr/ppermute | solution.py:11
  664.2 13.0 %collective-permute-start.2 = (f32[8,2,2,3,3,128]{5,4,3,2,1,0:T(4,128)S(1)}, f32[8,2,2,3,3,128]{5,4,3,2,1,0:T(4,128)S(1)}, u32[]{:S(2)}, u32[]{:S(2)}) collective-permute-start(f32[8,2,2,3,3,128]{5,4,3,2,1,0:T(4,128)S(1)} %get-tuple-element.580), channel_id=1, source_target_pairs={{496,0},{0,16},{16,32},{32,48},{48,64},{64,80},{80,96},{96,112},{1... | collective-permute-start | bytes 442376 | tf_op jit(solution)/shard_map/while/body/eval_jaxpr/ppermute | solution.py:11
  677.2 13.0 %collective-permute-start.2 = (f32[8,2,2,3,3,128]{5,4,3,2,1,0:T(4,128)S(1)}, f32[8,2,2,3,3,128]{5,4,3,2,1,0:T(4,128)S(1)}, u32[]{:S(2)}, u32[]{:S(2)}) collective-permute-start(f32[8,2,2,3,3,128]{5,4,3,2,1,0:T(4,128)S(1)} %get-tuple-element.580), channel_id=1, source_target_pairs={{496,0},{0,16},{16,32},{32,48},{48,64},{64,80},{80,96},{96,112},{1... | collective-permute-start | bytes 442376 | tf_op jit(solution)/shard_map/while/body/eval_jaxpr/ppermute | solution.py:11
  690.3 13.0 %collective-permute-start.2 = (f32[8,2,2,3,3,128]{5,4,3,2,1,0:T(4,128)S(1)}, f32[8,2,2,3,3,128]{5,4,3,2,1,0:T(4,128)S(1)}, u32[]{:S(2)}, u32[]{:S(2)}) collective-permute-start(f32[8,2,2,3,3,128]{5,4,3,2,1,0:T(4,128)S(1)} %get-tuple-element.580), channel_id=1, source_target_pairs={{496,0},{0,16},{16,32},{32,48},{48,64},{64,80},{80,96},{96,112},{1... | collective-permute-start | bytes 442376 | tf_op jit(solution)/shard_map/while/body/eval_jaxpr/ppermute | solution.py:11
  703.4 13.0 %collective-permute-start.2 = (f32[8,2,2,3,3,128]{5,4,3,2,1,0:T(4,128)S(1)}, f32[8,2,2,3,3,128]{5,4,3,2,1,0:T(4,128)S(1)}, u32[]{:S(2)}, u32[]{:S(2)}) collective-permute-start(f32[8,2,2,3,3,128]{5,4,3,2,1,0:T(4,128)S(1)} %get-tuple-element.580), channel_id=1, source_target_pairs={{496,0},{0,16},{16,32},{32,48},{48,64},{64,80},{80,96},{96,112},{1... | collective-permute-start | bytes 442376 | tf_op jit(solution)/shard_map/while/body/eval_jaxpr/ppermute | solution.py:11
  716.5 13.0 %collective-permute-start.2 = (f32[8,2,2,3,3,128]{5,4,3,2,1,0:T(4,128)S(1)}, f32[8,2,2,3,3,128]{5,4,3,2,1,0:T(4,128)S(1)}, u32[]{:S(2)}, u32[]{:S(2)}) collective-permute-start(f32[8,2,2,3,3,128]{5,4,3,2,1,0:T(4,128)S(1)} %get-tuple-element.580), channel_id=1, source_target_pairs={{496,0},{0,16},{16,32},{32,48},{48,64},{64,80},{80,96},{96,112},{1... | collective-permute-start | bytes 442376 | tf_op jit(solution)/shard_map/while/body/eval_jaxpr/ppermute | solution.py:11
  729.6 13.0 %collective-permute-start.2 = (f32[8,2,2,3,3,128]{5,4,3,2,1,0:T(4,128)S(1)}, f32[8,2,2,3,3,128]{5,4,3,2,1,0:T(4,128)S(1)}, u32[]{:S(2)}, u32[]{:S(2)}) collective-permute-start(f32[8,2,2,3,3,128]{5,4,3,2,1,0:T(4,128)S(1)} %get-tuple-element.580), channel_id=1, source_target_pairs={{496,0},{0,16},{16,32},{32,48},{48,64},{64,80},{80,96},{96,112},{1... | collective-permute-start | bytes 442376 | tf_op jit(solution)/shard_map/while/body/eval_jaxpr/ppermute | solution.py:11
  742.7 13.0 %collective-permute-start.2 = (f32[8,2,2,3,3,128]{5,4,3,2,1,0:T(4,128)S(1)}, f32[8,2,2,3,3,128]{5,4,3,2,1,0:T(4,128)S(1)}, u32[]{:S(2)}, u32[]{:S(2)}) collective-permute-start(f32[8,2,2,3,3,128]{5,4,3,2,1,0:T(4,128)S(1)} %get-tuple-element.580), channel_id=1, source_target_pairs={{496,0},{0,16},{16,32},{32,48},{48,64},{64,80},{80,96},{96,112},{1... | collective-permute-start | bytes 442376 | tf_op jit(solution)/shard_map/while/body/eval_jaxpr/ppermute | solution.py:11
  755.8 13.0 %collective-permute-start.2 = (f32[8,2,2,3,3,128]{5,4,3,2,1,0:T(4,128)S(1)}, f32[8,2,2,3,3,128]{5,4,3,2,1,0:T(4,128)S(1)}, u32[]{:S(2)}, u32[]{:S(2)}) collective-permute-start(f32[8,2,2,3,3,128]{5,4,3,2,1,0:T(4,128)S(1)} %get-tuple-element.580), channel_id=1, source_target_pairs={{496,0},{0,16},{16,32},{32,48},{48,64},{64,80},{80,96},{96,112},{1... | collective-permute-start | bytes 442376 | tf_op jit(solution)/shard_map/while/body/eval_jaxpr/ppermute | solution.py:11
  (39 other events, 962.7 us)
where the time goes:
time: 780 us; the launch traced here: 771 us
  local copies, waits for them, and re-layouts  177 us (23%)
  starting transfers between devices  171 us (22%)
  waiting for transfers between devices  160 us (21%)
  blocking collectives  100 us (13%)
  loops' own time  96.8 us (12%)
  other arithmetic  53.1 us (7%)
  matrix products  12.2 us (2%)
    ppermute x36, starting transfers between devices, from_behind(): return lax.ppermute(block, axis, route)  171 us
    ppermute x36, waiting for transfers between devices, from_behind(): return lax.ppermute(block, axis, route)  160 us
    psum x1, blocking collectives, per_device(): summed = lax.psum(partial_grad, ('gx', 'yz'))  100 us
    mul x364, local copies, waits for them, and re-layouts, matmul_three(): left[..., :, :, None, :] * right[..., None, :, :, :]  64.4 us
    another operation x1, loops' own time, per_device(): lax.scan(forward_step, gauge_links, offsets)  51.7 us
    another operation x1, loops' own time, per_device(): lax.scan(backward_step, accumulator, (offsets, line_grad, all_lines))  44 us
    dynamic_slice x48, local copies, waits for them, and re-layouts, per_device(): lax.scan(forward_step, gauge_links, offsets)  29.5 us
    squeeze x24, local copies, waits for them, and re-layouts, per_device(): lax.scan(backward_step, accumulator, (offsets, line_grad, all_lines))  22.2 us
  transfers between devices with their start and end apart: 36, of which 24 were waited for; matrix products, arithmetic and copies ran while one was open for 1% of the time, Pallas kernels for 0%

commit v1 on v0

--- a/solution.py
+++ b/solution.py
@@ -94,7 +94,7 @@
     grad_field = direct + far_terms
     total_x = part_x * lax.axis_size("gx")
     total_sites = site_count * lax.axis_size("yz")
-    summed = lax.psum(partial_grad, ("gx", "yz"))
+    summed = jnp.sum(lax.all_gather(partial_grad, ("gx", "yz")), axis=0)
     grad_weights = summed.reshape(channels, channels, line_count, channels) / math.sqrt(
         100.0 * total_x * total_sites
     )

time: 780 us -> 1980 us (2.54)
  the two profiles are of different devices: /device:TPU:2 before, /device:TPU:473 now
where the time goes in v1:
time: 1980 us; the launch traced here: 1970 us
  waiting for transfers between devices  1360 us (69%)
  local copies, waits for them, and re-layouts  216 us (11%)
  starting transfers between devices  164 us (8%)
  loops' own time  99 us (5%)
  other arithmetic  97.2 us (5%)
    all_gather x1, waiting for transfers between devices, per_device(): summed = jnp.sum(lax.all_gather(partial_grad, ('gx', 'yz')), axis=0)  1200 us
    ppermute x36, starting transfers between devices, from_behind(): return lax.ppermute(block, axis, route)  164 us
    ppermute x36, waiting for transfers between devices, from_behind(): return lax.ppermute(block, axis, route)  160 us
    mul x364, local copies, waits for them, and re-layouts, matmul_three(): left[..., :, :, None, :] * right[..., None, :, :, :]  97.3 us
    another operation x1, loops' own time, per_device(): lax.scan(backward_step, accumulator, (offsets, line_grad, all_lines))  49.8 us
    another operation x1, loops' own time, per_device(): lax.scan(forward_step, gauge_links, offsets)  48.2 us
  transfers between devices with their start and end apart: 37, of which 37 were waited for; matrix products, arithmetic and copies ran while one was open for 4% of the time, Pallas kernels for 0%

profile of v1, /device:TPU:473, one launch (start us, length us, event | category | flops | bytes accessed | tf_op | source)
XLA Modules:
  0.0 1967.3 jit_solution(2745664473801611769)
XLA Ops:
  12.6 177.0 %while.50 = (s32[]{:T(128)}, f32[2,2,3,3,128]{4,1,3,2,0:T(2,128)S(1)}, f32[8,2,2,3,3,128]{5,2,4,3,1,0:T(2,128)S(1)}, f32[12,2,2,3,3,128]{5,1,0,4,3,2:T(2,128)S(1...) while((s32[]{:T(128)}, f32[2,2,3,3,128]{4,1,3,2,0:T(2,128)S(1)}, ...), condition=%wide.region_1.2_spmd, body=%wide.region_0.1_spmd.sunk | while | flops 2 | bytes 1327269 | solution.py:46
  17.1 6.6 collective-permute-done
  23.7 3.9 collective-permute-done.1
  31.6 7.3 collective-permute-done
  46.3 7.3 collective-permute-done
  61.0 7.3 collective-permute-done
  75.8 7.3 collective-permute-done
  90.5 7.3 collective-permute-done
  105.2 7.3 collective-permute-done
  119.9 7.3 collective-permute-done
  134.6 7.3 collective-permute-done
  149.3 7.3 collective-permute-done
  164.1 7.3 collective-permute-done
  178.8 7.3 collective-permute-done
  193.3 259.2 %while.51 = (s32[]{:T(128)}, f32[2,2,3,3,128]{4,0,3,2,1:T(2,128)}, f32[24,8,2,2,3,3,128]{6,1,5,4,3,2,0:T(8,128)S(1)}, f32[24,2,2,3,3,128]{5,1,4,3,2,0:T(2,128)},...) while((s32[]{:T(128)}, f32[2,2,3,3,128]{4,0,3,2,1:T(2,128)}, ...), condition=%wide.region_15.16_spmd, body=%wide.region_2.15_spmd.sunk | while | flops 910086 | bytes 2894023 | solution.py:63
  466.1 4.2 fusion.7
  470.3 6.0 fusion.6
  476.4 110.9 %while.52 = (s32[]{:T(128)}, f32[8,26,2,3,3,128]{5,0,4,3,2,1:T(8,128)S(1)}, s32[24]{0:T(128)S(1)}, f32[24,2,2,3,3,128]{5,1,4,3,2,0:T(2,128)}, f32[24,8,2,2,3,3,1...) while((s32[]{:T(128)}, f32[8,26,2,3,3,128]{5,0,4,3,2,1:T(8,128)S(1)}, s32[24]{0:T(128)S(1)}, ...), condition=%wide.region_34.35_spmd, body=%wide.region_25.34_spmd.sunk | while | flops 891653 | bytes 3410075 | solution.py:84
  591.9 150.0 %while.53 = (s32[]{:T(128)}, f32[8,2,2,3,3,128]{5,4,3,2,1,0:T(4,128)S(1)}, f32[12,8,2,2,3,3,128]{6,1,5,4,3,2,0:T(8,128)S(1)}, s32[]{:T(128)}) while((s32[]{:T(128)}, f32[8,2,2,3,3,128]{5,4,3,2,1,0:T(4,128)S(1)}, f32[12,8,2,2,3,3,128]{6,1,5,4,3,2,0:T(8,128)S(1)}, s32[]{:T(128)}) %tuple.162), condition=%wide.region_36.37_spmd, body=%wide.region_35.36_spmd.sunk | while | flops 36866 | bytes 1327209 | solution.py:93
  596.7 10.5 collective-permute-start.2
  610.0 10.4 collective-permute-start.2
  623.3 10.5 collective-permute-start.2
  636.6 10.4 collective-permute-start.2
  649.8 10.4 collective-permute-start.2
  663.0 10.4 collective-permute-start.2
  676.2 10.4 collective-permute-start.2
  689.3 10.5 collective-permute-start.2
  702.5 10.5 collective-permute-start.2
  715.6 10.5 collective-permute-start.2
  728.8 10.5 collective-permute-start.2
  742.7 1203.5 %all-gather.3.cloned.1.call-done = f32[32768,192]{1,0:T(8,128)} async-done(((f32[64,192]{1,0:T(8,128)}), f32[32768,192]{1,0:T(8,128)}) %all-gather.3.cloned.1.call-update) | async-done | bytes 25165840 | tf_op jit(solution)/shard_map/all_gather | solution.py:97
  1946.3 12.9 reduce_sum.279
  (1166 shorter events, 422.0 us)
Async XLA Ops:
  7.2 1939.1 %all-gather.3.cloned.1.call-start = ((), (), s32[]{:S(2)}) async-start(), calls=%async_computation | async-start | bytes 33619968 | tf_op jit(solution)/shard_map/all_gather | solution.py:97
  15.2 12.5 collective-permute-start.1
  27.8 11.1 collective-permute-start
  29.7 12.7 collective-permute-start.1
  44.4 12.7 collective-permute-start.1
  57.2 11.1 collective-permute-start
  59.1 12.7 collective-permute-start.1
  71.9 11.1 collective-permute-start
  73.8 12.7 collective-permute-start.1
  88.5 12.7 collective-permute-start.1
  101.3 11.1 collective-permute-start
  103.3 12.7 collective-permute-start.1
  116.1 11.1 collective-permute-start
  118.0 12.7 collective-permute-start.1
  130.8 11.1 collective-permute-start
  132.7 12.7 collective-permute-start.1
  145.5 11.1 collective-permute-start
  147.4 12.7 collective-permute-start.1
  160.2 11.1 collective-permute-start
  162.1 12.7 collective-permute-start.1
  176.9 12.7 collective-permute-start.1
  596.7 13.3 collective-permute-start.2
  610.0 13.2 collective-permute-start.2
  623.3 13.2 collective-permute-start.2
  636.6 13.1 collective-permute-start.2
  649.8 13.1 collective-permute-start.2
  663.0 13.1 collective-permute-start.2
  676.2 13.0 collective-permute-start.2
  689.3 13.1 collective-permute-start.2
  702.5 13.1 collective-permute-start.2
  715.6 13.1 collective-permute-start.2
  728.8 13.1 collective-permute-start.2
  (15 other events, 241.9 us)
Sparse Core Ops, SparseCore 0:
  470.4 1475.8 all-gather.2
